TPU v7x, 256 devices: a whole 4x4x8 slice. The times are simulated.
256 devices in a mesh: section: 16 (over y_hi, x, core), ray: 8 (over z), dp: 2 (over y_lo).
Axes of the slice: x: 4, y: 4 (y_hi: 2, y_lo: 2; y = y_hi * 2 + y_lo), z: 8, core: 2. Of those that a mesh axis runs over, the one named last changes fastest.
Arguments:
- section_tokens: bfloat16 [16, 2, 1024, 1024], P('section', 'dp', 'ray'), may hold values from -6 to 6
- enc_ln1: float32 [16, 1024], P('section'), may hold values from 0.5 to 1.5
- enc_qkv: bfloat16 [16, 1024, 3, 1024], P('section', None, None, 'ray'), may hold values from -40 to 40
- enc_out: bfloat16 [16, 1024, 1024], P('section', 'ray'), may hold values from -0.1875 to 0.1875
- enc_ln2: float32 [16, 1024], P('section'), may hold values from 0.5 to 1.5
- enc_up: bfloat16 [16, 1024, 4096], P('section', None, 'ray'), may hold values from -0.1875 to 0.1875
- enc_down: bfloat16 [16, 4096, 1024], P('section', 'ray'), may hold values from -0.09375 to 0.09375
- set_latent: bfloat16 [2, 1024, 1024], P('dp', 'ray'), may hold values from -6 to 6
- ray_queries: bfloat16 [2, 32768, 1024], P('dp', ('section', 'ray')), may hold values from -6 to 6
- dec_query: bfloat16 [1024, 1024], P('section'), may hold values from -40 to 40
- dec_kv: bfloat16 [1024, 2, 1024], P('section'), may hold values from -1 to 1
- dec_out: bfloat16 [1024, 1024], P('section'), may hold values from -0.1875 to 0.1875
- feature_grad: bfloat16 [2, 32768, 1024], P('dp', ('section', 'ray')), may hold values from -2 to 2
Outputs:
- handed: bfloat16 [16, 2, 1024, 1024], P('section', 'dp', 'ray')
- finished: bfloat16 [2, 1024, 1024], P('dp', 'ray', 'section')
- ray_features: bfloat16 [2, 32768, 1024], P('dp', ('section', 'ray'))
- latent_grad: bfloat16 [2, 1024, 1024], P('dp', 'ray')
- out_grad: float32 [1024, 1024], replicated
All inputs are finite; a program needn't handle non-finite values.
Results may differ from a plain program's by a relative error of at most 0.022.
The roundings to bfloat16 on the way count: a program that leaves them out, or rounds other values in their place, can miss the bound.
Values may be sent and summed in bfloat16 or wider, within the bound.
No kernel may reach another device: no remote copies, remote signals or barrier semaphores. Data moves between devices by JAX's collectives and lax.ppermute only.
A program may use at most 128 MiB of HBM per device.

v0:
```python
import math
import jax
import jax.numpy as jnp
from jax import lax
from jax.sharding import PartitionSpec as P

HEADS = 16


def shifted(value, axis, by):
    count = lax.axis_size(axis)
    pairs = [(i, i + by) for i in range(count) if 0 <= i + by < count]
    return lax.ppermute(value, axis, pairs)


def spread_2(value, axis, root):
    mine = lax.axis_index(axis) == root
    return lax.psum(jnp.where(mine, value, jnp.zeros_like(value)), axis)


def layer_norm(values, gain):
    values = values.astype(jnp.float32)
    center = values - jnp.mean(values, -1, keepdims=True)
    spread = jnp.mean(center * center, -1, keepdims=True)
    return center * lax.rsqrt(spread + 1e-05) * gain


def softmax_rows(scores):
    top = jnp.max(scores, -1, keepdims=True)
    expo = jnp.exp(scores - top)
    return expo / jnp.sum(expo, -1, keepdims=True)


def attend_heads(packed, head_dim):
    length = packed.shape[0]
    heads = packed.shape[1] // (3 * head_dim)
    split = packed.reshape(length, 3, heads, head_dim)
    scores = jnp.einsum(
        "qhd,khd->hqk", split[:, 0], split[:, 1], preferred_element_type=jnp.float32
    ) / math.sqrt(head_dim)
    probs = softmax_rows(scores).astype(jnp.bfloat16)
    mixed = jnp.einsum("hqk,khd->qhd", probs, split[:, 2], preferred_element_type=jnp.float32)
    return mixed.astype(jnp.bfloat16).reshape(length, heads * head_dim)


def latent_rows(pair_sum, w_pairs):
    result = lax.dot_general(
        pair_sum[:, 0],
        w_pairs[:, 0, :],
        (((1,), (1,)), ((), ())),
        preferred_element_type=jnp.float32,
    )
    result = result + lax.dot_general(
        pair_sum[:, 1],
        w_pairs[:, 1, :],
        (((1,), (1,)), ((), ())),
        preferred_element_type=jnp.float32,
    )
    return result.astype(jnp.bfloat16)


def local(
    section_tokens,
    enc_ln1,
    enc_qkv,
    enc_out,
    enc_ln2,
    enc_up,
    enc_down,
    set_latent,
    ray_queries,
    dec_query,
    dec_kv,
    dec_out,
    feature_grad,
):
    tokens = section_tokens[0, 0]
    width = tokens.shape[1]
    head_dim = width // HEADS
    local_width = enc_out.shape[1]
    w_qkv = enc_qkv[0].reshape(width, 3 * local_width)
    w_attn_out = enc_out[0]
    w_upper = enc_up[0]
    w_lower = enc_down[0]
    gain_one = enc_ln1[0]
    gain_two = enc_ln2[0]
    normed = layer_norm(tokens, gain_one).astype(jnp.bfloat16)
    packed = jnp.dot(
        lax.all_gather(normed, "ray", axis=0, tiled=True), w_qkv, preferred_element_type=jnp.float32
    ).astype(jnp.bfloat16)
    mixed = attend_heads(packed, head_dim)
    attn_rows = lax.psum_scatter(
        jnp.dot(mixed, w_attn_out, preferred_element_type=jnp.float32).astype(jnp.bfloat16),
        "ray",
        scatter_dimension=0,
        tiled=True,
    ).astype(jnp.float32)
    hidden = (tokens.astype(jnp.float32) + attn_rows).astype(jnp.bfloat16)
    upper = jax.nn.gelu(
        jnp.dot(
            lax.all_gather(
                layer_norm(hidden, gain_two).astype(jnp.bfloat16), "ray", axis=0, tiled=True
            ),
            w_upper,
            preferred_element_type=jnp.float32,
        ),
        approximate=True,
    ).astype(jnp.bfloat16)
    lower_rows = lax.psum_scatter(
        jnp.dot(upper, w_lower, preferred_element_type=jnp.float32).astype(jnp.bfloat16),
        "ray",
        scatter_dimension=0,
        tiled=True,
    ).astype(jnp.float32)
    layer_out = (hidden.astype(jnp.float32) + lower_rows).astype(jnp.bfloat16)
    handed = shifted(layer_out, "section", 1)
    finished_all = spread_2(layer_out, "section", lax.axis_size("section") - 1)
    columns = width // lax.axis_size("section")
    finished = lax.dynamic_slice_in_dim(
        finished_all, lax.axis_index("section") * columns, columns, 1
    )
    w_query, w_pairs, w_mix = (
        lax.all_gather(dec_query, "section", axis=0, tiled=True),
        lax.all_gather(dec_kv, "section", axis=0, tiled=True),
        lax.all_gather(dec_out, "section", axis=0, tiled=True),
    )
    latent = set_latent[0]
    queries = ray_queries[0]
    cotangent = feature_grad[0]
    flat_pairs = w_pairs.reshape(width, 2 * width)
    key_values = lax.all_gather(
        jnp.dot(latent, flat_pairs, preferred_element_type=jnp.float32).astype(jnp.bfloat16),
        "ray",
        axis=0,
        tiled=True,
    )
    scene_len = key_values.shape[0]
    ray_rows = queries.shape[0]
    scale = 1.0 / math.sqrt(head_dim)
    keys = key_values[:, :width].reshape(scene_len, HEADS, head_dim)
    values = key_values[:, width:].reshape(scene_len, HEADS, head_dim)
    query = (
        jnp.dot(queries, w_query, preferred_element_type=jnp.float32)
        .astype(jnp.bfloat16)
        .reshape(ray_rows, HEADS, head_dim)
    )
    scores = jnp.einsum("rhd,lhd->hrl", query, keys, preferred_element_type=jnp.float32) * scale
    probs = softmax_rows(scores)
    probs_low = probs.astype(jnp.bfloat16)
    attended = (
        jnp.einsum("hrl,lhd->rhd", probs_low, values, preferred_element_type=jnp.float32)
        .astype(jnp.bfloat16)
        .reshape(ray_rows, width)
    )
    features = (
        queries.astype(jnp.float32) + jnp.dot(attended, w_mix, preferred_element_type=jnp.float32)
    ).astype(jnp.bfloat16)
    mix_term = lax.dot_general(
        attended, cotangent, (((0,), (0,)), ((), ())), preferred_element_type=jnp.float32
    )
    out_grad = lax.psum(mix_term, ("section", "ray", "dp"))
    attn_grad = lax.dot_general(
        cotangent, w_mix, (((1,), (1,)), ((), ())), preferred_element_type=jnp.float32
    )
    attn_grad = attn_grad.astype(jnp.bfloat16).reshape(ray_rows, HEADS, head_dim)
    prob_grad = jnp.einsum("rhd,lhd->hrl", attn_grad, values, preferred_element_type=jnp.float32)
    delta = jnp.sum(probs * prob_grad, -1, keepdims=True)
    score_grad = (probs * (prob_grad - delta) * scale).astype(jnp.bfloat16)
    count = latent.shape[0] * lax.axis_size("ray")
    key_grad = jnp.einsum(
        "hrl,rhd->lhd", score_grad, query, preferred_element_type=jnp.float32
    ).reshape(count, width)
    value_grad = jnp.einsum(
        "hrl,rhd->lhd", probs_low, attn_grad, preferred_element_type=jnp.float32
    ).reshape(count, width)
    stacked = jnp.stack([key_grad, value_grad], 1)
    pair_rows = lax.psum_scatter(
        stacked.astype(jnp.bfloat16), "ray", scatter_dimension=0, tiled=True
    )
    pair_sum = lax.psum(pair_rows, "section")
    latent_grad = latent_rows(pair_sum, w_pairs)
    return (handed[None, None], finished[None], features[None], latent_grad[None], out_grad)


def solution(mesh):
    return jax.shard_map(
        local,
        mesh=mesh,
        in_specs=(
            P("section", "dp", "ray", None),
            P("section", None),
            P("section", None, None, "ray"),
            P("section", "ray", None),
            P("section", None),
            P("section", None, "ray"),
            P("section", "ray", None),
            P("dp", "ray", None),
            P("dp", ("section", "ray"), None),
            P("section", None),
            P("section", None, None),
            P("section", None),
            P("dp", ("section", "ray"), None),
        ),
        out_specs=(
            P("section", "dp", "ray", None),
            P("dp", "ray", "section"),
            P("dp", ("section", "ray"), None),
            P("dp", "ray", None),
            P(),
        ),
        check_vma=False,
    )
```

profile of v0, /device:TPU:2, one launch (start us, length us, event | category | flops | bytes accessed | tf_op | source)
XLA Modules:
  0.0 928.3 jit_solution(4946242236666145838)
XLA Ops:
  8.1 1.1 convert_reduce_fusion.1
  9.2 1.2 fusion.73
  10.4 1.9 fusion.75
  12.4 1.4 copy.44
  13.8 42.5 %all-gather.7.cloned.1.call-done = bf16[1024,1024]{1,0:T(8,128)(2,1)} async-done(((bf16[128,1024]{1,0:T(8,128)(2,1)}), bf16[1024,1024]{1,0:T(8,128)(2,1)}) %all-gather.7.cloned.1.call-update) | async-done | bytes 2097168 | tf_op jit(solution)/shard_map/all_gather | solution.py:89
  56.3 2.6 convolution_convert_fusion.3
  58.9 4.9 fusion.97
  63.7 4.3 fusion.48
  68.1 2.1 convolution_convert_fusion.2
  71.9 39.7 %reduce-scatter.6.cloned.1.call-done = bf16[128,1024]{1,0:T(8,128)(2,1)} async-done(((bf16[1024,1024]{1,0:T(8,128)(2,1)}), bf16[128,1024]{1,0:T(8,128)(2,1)}) %reduce-scatter.6.cloned.1.call-update) | async-done | bytes 262160 | tf_op jit(solution)/shard_map/reduce_scatter | solution.py:92
  111.7 1.1 convert_reduce_fusion
  113.0 0.9 fusion.72
  114.0 18.6 %all-gather.11.cloned.1.call-done = bf16[1024,2,1024]{2,1,0:T(2,128)(2,1)} async-done(((bf16[64,2,1024]{2,1,0:T(2,128)(2,1)}), bf16[1024,2,1024]{2,1,0:T(2,128)(2,1)}) %all-gather.11.cloned.1.call-update) | async-done | bytes 4194320 | tf_op jit(solution)/shard_map/all_gather | solution.py:124
  132.7 11.1 %copy.47 = bf16[1024,2,1024]{0,2,1:T(8,128)(2,1)} copy(bf16[1024,2,1024]{2,1,0:T(2,128)(2,1)} %all-gather.11.cloned.1.call-done) | data formatting | bytes 8388608 | tf_op jit(solution)/shard_map/all_gather | solution.py:124
  143.8 4.6 convolution_convert_fusion
  148.5 39.0 %all-gather.15.cloned.1.call-done = bf16[1024,1024]{1,0:T(8,128)(2,1)} async-done(((bf16[64,1024]{1,0:T(8,128)(2,1)}), bf16[1024,1024]{1,0:T(8,128)(2,1)}) %all-gather.15.cloned.1.call-update) | async-done | bytes 2097168 | tf_op jit(solution)/shard_map/all_gather | solution.py:123
  187.5 2.3 convolution_convert_fusion.5
  189.8 1.0 copy.49
  190.8 51.5 %all-gather.17.cloned.1.call-done = bf16[1024,1024]{1,0:T(8,128)(2,1)} async-done(((bf16[64,1024]{1,0:T(8,128)(2,1)}), bf16[1024,1024]{1,0:T(8,128)(2,1)}) %all-gather.17.cloned.1.call-update) | async-done | bytes 2097168 | tf_op jit(solution)/shard_map/all_gather | solution.py:125
  242.3 2.3 convolution_convert_fusion.4
  244.6 1.0 copy.51
  245.6 39.2 %all-gather.9.cloned.1.call-done = bf16[1024,1024]{1,0:T(8,128)(2,1)} async-done(((bf16[128,1024]{1,0:T(8,128)(2,1)}), bf16[1024,1024]{1,0:T(8,128)(2,1)}) %all-gather.9.cloned.1.call-update) | async-done | bytes 2097168 | tf_op jit(solution)/shard_map/all_gather | solution.py:101
  284.9 5.8 convolution_convert_fusion.1
  290.9 66.2 %all-gather.13.cloned.1.call-done = bf16[1024,2048]{1,0:T(8,128)(2,1)} async-done(((bf16[128,2048]{1,0:T(8,128)(2,1)}), bf16[1024,2048]{1,0:T(8,128)(2,1)}) %all-gather.13.cloned.1.call-update) | async-done | bytes 4194320 | tf_op jit(solution)/shard_map/all_gather | solution.py:131
  357.2 4.0 fusion.96
  361.2 2.6 copy.50
  363.8 2.9 copy.48
  366.7 9.8 %fusion.98 = (f32[16,256]{1,0:T(8,128)S(1)}, f32[16,256,1024]{2,1,0:T(8,128)}) fusion(bf16[256,16,64]{0,2,1:T(8,128)(2,1)S(1)} %bitcast.149, bf16[1024,16,64]{0,2,1:T(8,128)(2,1)} %bitcast.144), kind=kOutput, calls=%fused_computation.110 | convolution fusion | flops 549454848 | bytes 19415040 | tf_op jit(solution)/shard_map/sub | solution.py:30
  376.5 8.1 fusion.99
  384.5 38.2 %fusion.38 = bf16[16,64,1024]{2,1,0:T(8,128)(2,1)} fusion(bf16[256,16,64]{0,2,1:T(8,128)(2,1)S(1)} %bitcast.150, f32[16,256,1024]{2,1,0:T(8,128)} %fusion.99, f32[16,256,1024]{2,1,0:T(8,128)} %get-tuple-element.18, f32[16,256]{1,0:T(8,128)S(1)} %get-tuple-element.17), kind=kOutput, calls=%fused_computation.40 | convolution fusion | flops 567284736 | bytes 36192256 | tf_op jit(solution)/shard_map/hrl,rhd->lhd/dot_general | solution.py:170
  422.8 7.1 fusion.35
  429.9 2.4 pad_maximum_fusion
  432.3 6.5 copy.57
  438.9 1.9 broadcast_select_fusion
  440.8 52.2 %reduce-scatter.10.cloned.1.call-done = bf16[128,2048]{1,0:T(8,128)(2,1)} async-done(((bf16[1024,2048]{1,0:T(8,128)(2,1)}), bf16[128,2048]{1,0:T(8,128)(2,1)}) %reduce-scatter.10.cloned.1.call-update) | async-done | bytes 524304
  492.9 2.0 copy.58
  495.3 8.5 fusion.42
  503.8 2.7 fusion.78
  506.5 10.0 %fusion.95 = (bf16[1024,1,1024]{2,1,0:T(2,128)(2,1)}, bf16[1024,1,1024]{2,1,0:T(2,128)(2,1)}) fusion(bf16[1024,2,1024]{2,1,0:T(2,128)(2,1)} %all-gather.11.cloned.1.call-done), kind=kLoop, calls=%fused_computation.107 | loop fusion | bytes 8388608 | tf_op jit(solution)/shard_map/slice | solution.py:49
  516.5 1.9 collective-permute-start
  518.5 1.5 fusion.45
  520.0 4.7 collective-permute-done
  524.7 109.9 %all-reduce.6.cloned.1.call-done = (bf16[128,1024]{1,0:T(8,128)(2,1)}, bf16[128,2,1024]{0,2,1:T(8,128)(2,1)}) async-done(((bf16[128,1024]{1,0:T(8,128)(2,1)}, bf16[128,2,1024]{0,2,1:T(8,128)(2,1)}), (bf16[128,1024]{1,0:T(8,128)(2,1)}, bf16[128,2,1024]{0,2,1:T(8,128)(2,1)})) %all-reduce.6.cloned.1.call-update) | async-done | bytes 786448 | tf_op jit(solution)/shard_map/psum | solution.py:18
  634.6 0.8 constant_dynamic-slice_fusion
  636.2 3.1 fusion.33
  639.3 3.9 fusion.49
  643.2 272.5 %all-reduce.4.cloned.1.call-done = f32[1024,1024]{1,0:T(8,128)} async-done(((f32[1024,1024]{1,0:T(8,128)}), f32[1024,1024]{1,0:T(8,128)}) %all-reduce.4.cloned.1.call-update) | async-done | bytes 4194320 | tf_op jit(solution)/shard_map/psum | solution.py:161
  916.4 4.8 copy.76
  (60 shorter events, 4.3 us)
Async XLA Ops:
  8.0 276.9 %copy-start = (bf16[1,512,1024]{2,1,0:T(8,128)(2,1)S(1)}, bf16[1,512,1024]{2,1,0:T(8,128)(2,1)}, u32[]{:S(2)}) copy-start(bf16[1,512,1024]{2,1,0:T(8,128)(2,1)} %param.19) | copy-start | bytes 3145732
  8.0 48.2 %all-gather.7.cloned.1.call-start = ((), (), s32[]{:S(2)}) async-start(), calls=%async_computation.3 | async-start | bytes 2359296 | tf_op jit(solution)/shard_map/all_gather | solution.py:89
  12.3 99.4 %reduce-scatter.6.cloned.1.call-start = ((), (), s32[]{:S(2)}) async-start(), calls=%async_computation.4 | async-start | bytes 2359296 | tf_op jit(solution)/shard_map/reduce_scatter | solution.py:92
  63.7 4.3 copy-start.11
  68.0 43.6 %copy-start.2 = (bf16[1,1,128,1024]{3,2,1,0:T(8,128)(2,1)S(1)}, bf16[1,1,128,1024]{3,2,1,0:T(8,128)(2,1)}, u32[]{:S(2)}) copy-start(bf16[1,1,128,1024]{3,2,1,0:T(8,128)(2,1)} %param.13) | copy-start | bytes 786436
  68.0 45.0 %copy-start.14 = (f32[1,1024]{1,0:T(1,128)S(1)}, f32[1,1024]{1,0:T(1,128)}, u32[]{:S(2)}) copy-start(f32[1,1024]{1,0:T(1,128)} %param.17) | copy-start | bytes 12292
  70.1 62.5 %all-gather.11.cloned.1.call-start = ((), (), s32[]{:S(2)}) async-start(), calls=%async_computation.7 | async-start | bytes 4456448 | tf_op jit(solution)/shard_map/all_gather | solution.py:124
  70.7 116.8 %all-gather.15.cloned.1.call-start = ((), (), s32[]{:S(2)}) async-start(), calls=%async_computation.9 | async-start | bytes 2228224 | tf_op jit(solution)/shard_map/all_gather | solution.py:123
  71.3 171.0 %all-gather.17.cloned.1.call-start = ((), (), s32[]{:S(2)}) async-start(), calls=%async_computation.10 | async-start | bytes 2228224 | tf_op jit(solution)/shard_map/all_gather | solution.py:125
  71.9 213.0 %all-gather.9.cloned.1.call-start = ((), (), s32[]{:S(2)}) async-start(), calls=%async_computation.5 | async-start | bytes 2359296 | tf_op jit(solution)/shard_map/all_gather | solution.py:101
  114.0 29.8 %copy-start.12 = (bf16[1,128,1024]{2,1,0:T(8,128)(2,1)S(1)}, bf16[1,128,1024]{2,1,0:T(8,128)(2,1)}, u32[]{:S(2)}) copy-start(bf16[1,128,1024]{2,1,0:T(8,128)(2,1)} %param.20) | copy-start | bytes 786436
  114.0 243.2 %all-gather.13.cloned.1.call-start = ((), (), s32[]{:S(2)}) async-start(), calls=%async_computation.8 | async-start | bytes 4718592 | tf_op jit(solution)/shard_map/all_gather | solution.py:131
  143.8 43.7 %copy-start.8 = (bf16[1,256,1024]{2,1,0:T(8,128)(2,1)S(1)}, bf16[1,256,1024]{2,1,0:T(8,128)(2,1)}, u32[]{:S(2)}) copy-start(bf16[1,256,1024]{2,1,0:T(8,128)(2,1)} %param.21) | copy-start | bytes 1572868
  143.8 98.5 %copy-start.6 = (bf16[1,256,1024]{2,1,0:T(8,128)(2,1)S(1)}, bf16[1,256,1024]{2,1,0:T(8,128)(2,1)}, u32[]{:S(2)}) copy-start(bf16[1,256,1024]{2,1,0:T(8,128)(2,1)} %param.25) | copy-start | bytes 1572868
  148.5 290.5 %reduce-scatter.8.cloned.1.call-start = ((), (), s32[]{:S(2)}) async-start(), calls=%async_computation.6 | async-start | bytes 2359296 | tf_op jit(solution)/shard_map/reduce_scatter | solution.py:109
  290.7 202.2 %reduce-scatter.10.cloned.1.call-start = ((), (), s32[]{:S(2)}) async-start(), calls=%async_computation.12 | async-start | bytes 4718592
  361.2 5.4 copy-start.10
  366.6 9.8 %copy-start.4 = (bf16[256,1024]{0,1:T(8,128)(2,1)S(1)}, bf16[256,1024]{0,1:T(8,128)(2,1)}, u32[]{:S(2)}) copy-start(bf16[256,1024]{0,1:T(8,128)(2,1)} %copy.51) | copy-start | bytes 1572868
  422.8 7.1 copy-start.5
  438.8 195.8 %all-reduce.6.cloned.1.call-start = ((), (), s32[]{:S(2)}) async-start(), calls=%async_computation.13 | async-start | bytes 1572864 | tf_op jit(solution)/shard_map/psum | solution.py:18
  495.0 8.8 copy-start.7
  495.0 420.7 %all-reduce.4.cloned.1.call-start = ((), (), s32[]{:S(2)}) async-start(), calls=%async_computation.11 | async-start | bytes 8388608 | tf_op jit(solution)/shard_map/psum | solution.py:161
  506.5 10.0 %copy-start.13 = (bf16[128,1024]{1,0:T(8,128)(2,1)S(1)}, bf16[128,1024]{1,0:T(8,128)(2,1)}, u32[]{:S(2)}) copy-start(bf16[128,1024]{1,0:T(8,128)(2,1)} %get-tuple-element.8) | copy-start | bytes 786436
  506.5 11.9 %copy-start.3 = (bf16[1024,1024]{1,0:T(8,128)(2,1)S(1)}, bf16[1024,1024]{1,0:T(8,128)(2,1)}, u32[]{:S(2)}) copy-start(bf16[1024,1024]{1,0:T(8,128)(2,1)} %all-gather.17.cloned.1.call-done) | copy-start | bytes 6291460
  506.5 11.9 %copy-start.9 = (bf16[1,256,1024]{2,1,0:T(8,128)(2,1)S(1)}, bf16[1,256,1024]{2,1,0:T(8,128)(2,1)}, u32[]{:S(2)}) copy-start(bf16[1,256,1024]{2,1,0:T(8,128)(2,1)} %param.21) | copy-start | bytes 1572868
  516.5 8.2 collective-permute-start
  915.7 5.5 copy-start.1
Sparse Core Ops, SparseCore 0:
  12.4 43.7 all-gather.6
  70.3 41.3 reduce-scatter.5
  290.8 69.1 reduce-scatter.7
  439.0 53.9 reduce-scatter.9
Sparse Core Ops, SparseCore 1:
  73.4 59.3 all-gather.10
  135.3 52.1 all-gather.14
  190.1 52.1 all-gather.16
  244.7 40.1 all-gather.8
  286.7 70.4 all-gather.12
  495.1 139.5 all-reduce.5
  640.0 275.7 all-reduce.3
where the time goes:
time: 929 us; the launch traced here: 928 us
  waiting for transfers between devices  738 us (79%)
  matrix products  112 us (12%)
  local copies, waits for them, and re-layouts  49.6 us (5%)
  between operations  15.6 us (2%)
  other arithmetic  10.7 us (1%)
    psum x1, waiting for transfers between devices, local(): out_grad = lax.psum(mix_term, ('section', 'ray', 'dp'))  273 us
    psum x1, waiting for transfers between devices, spread_2(): return lax.psum(jnp.where(mine, value, jnp.zeros_like(value)), axis)  110 us
    all_gather x1, waiting for transfers between devices, local(): lax.all_gather(jnp.dot(latent, flat_pairs, preferred_element_type=jnp.flo...  66.2 us
    unnamed x12, waiting for transfers between devices  53.9 us
    all_gather x1, waiting for transfers between devices, local(): lax.all_gather(dec_out, 'section', axis=0, tiled=True)  51.5 us
    all_gather x1, waiting for transfers between devices, local(): lax.all_gather(normed, 'ray', axis=0, tiled=True)  42.5 us
    reduce_scatter x1, waiting for transfers between devices, local(): lax.psum_scatter(jnp.dot(mixed, w_attn_out, preferred_element_type=jnp.fl...  39.7 us
    all_gather x1, waiting for transfers between devices, local(): lax.all_gather(layer_norm(hidden, gain_two).astype(jnp.bfloat16), 'ray',...  39.2 us
  transfers between devices with their start and end apart: 12, of which 11 were waited for; matrix products, arithmetic and copies ran while one was open for 16% of the time, Pallas kernels for 0%

commit v1 on v0

--- a/solution.py
+++ b/solution.py
@@ -128,11 +128,21 @@
     queries = ray_queries[0]
     cotangent = feature_grad[0]
     flat_pairs = w_pairs.reshape(width, 2 * width)
-    key_values = lax.all_gather(
-        jnp.dot(latent, flat_pairs, preferred_element_type=jnp.float32).astype(jnp.bfloat16),
-        "ray",
+    key_values = jnp.concatenate(
+        lax.all_to_all(
+            jnp.stack(
+                [
+                    jnp.dot(latent, flat_pairs, preferred_element_type=jnp.float32).astype(
+                        jnp.bfloat16
+                    )
+                ]
+                * lax.axis_size("ray")
+            ),
+            "ray",
+            0,
+            0,
+        ),
         axis=0,
-        tiled=True,
     )
     scene_len = key_values.shape[0]
     ray_rows = queries.shape[0]

time: 929 us -> 941 us (1.013)
    all_gather x1 -> x0, waiting for transfers between devices: 66.2 us -> none  [local(): lax.all_gather(jnp.dot(latent, flat_pairs, preferred_element_type=jnp.flo...]
    all_gather x1, waiting for transfers between devices: 18.6 us -> 47.3 us  [local(): lax.all_gather(dec_kv, 'section', axis=0, tiled=True)]
    all_gather x1, waiting for transfers between devices: 39 us -> 64.6 us  [local(): lax.all_gather(dec_query, 'section', axis=0, tiled=True)]
    unnamed x12 -> x11, waiting for transfers between devices: 53.9 us -> 54 us
  transfers between devices with their start and end apart: 12 -> 12, of which waited for: 11 -> 10; matrix products, arithmetic and copies ran while one was open for 16% -> 18% of each run, Pallas kernels for 0% -> 0%
where the time goes in v1:
time: 941 us; the launch traced here: 940 us
  waiting for transfers between devices  735 us (78%)
  matrix products  111 us (12%)
  local copies, waits for them, and re-layouts  58.9 us (6%)
  between operations  14.4 us (2%)
  other arithmetic  10.7 us (1%)
  starting transfers between devices  9.87 us (1%)
    psum x1, waiting for transfers between devices, local(): out_grad = lax.psum(mix_term, ('section', 'ray', 'dp'))  273 us
    psum x1, waiting for transfers between devices, spread_2(): return lax.psum(jnp.where(mine, value, jnp.zeros_like(value)), axis)  111 us
    all_gather x1, waiting for transfers between devices, local(): lax.all_gather(dec_query, 'section', axis=0, tiled=True)  64.6 us
    unnamed x11, waiting for transfers between devices  54 us
    all_gather x1, waiting for transfers between devices, local(): lax.all_gather(dec_out, 'section', axis=0, tiled=True)  51.6 us
    reduce_scatter x1, waiting for transfers between devices, local(): lax.psum_scatter(jnp.dot(mixed, w_attn_out, preferred_element_type=jnp.fl...  48.4 us
    all_gather x1, waiting for transfers between devices, local(): lax.all_gather(dec_kv, 'section', axis=0, tiled=True)  47.3 us
    all_gather x1, waiting for transfers between devices, local(): lax.all_gather(normed, 'ray', axis=0, tiled=True)  41.7 us
  transfers between devices with their start and end apart: 12, of which 10 were waited for; matrix products, arithmetic and copies ran while one was open for 18% of the time, Pallas kernels for 0%

profile of v1, /device:TPU:2, one launch (start us, length us, event | category | flops | bytes accessed | tf_op | source)
XLA Modules:
  0.0 940.1 jit_solution(16832324734643940970)
XLA Ops:
  7.2 1.1 convert_reduce_fusion.1
  8.4 1.2 fusion.73
  9.6 1.9 fusion.75
  12.3 1.4 copy.49
  13.7 41.7 %all-gather.6.cloned.1.call-done = bf16[1024,1024]{1,0:T(8,128)(2,1)} async-done(((bf16[128,1024]{1,0:T(8,128)(2,1)}), bf16[1024,1024]{1,0:T(8,128)(2,1)}) %all-gather.6.cloned.1.call-update) | async-done | bytes 2097168 | tf_op jit(solution)/shard_map/all_gather | solution.py:89
  55.4 2.6 convolution_convert_fusion.3
  58.0 4.9 fusion.97
  62.9 4.3 fusion.48
  67.2 2.1 convolution_convert_fusion.2
  70.5 47.3 %all-gather.10.cloned.1.call-done = bf16[1024,2,1024]{2,1,0:T(2,128)(2,1)} async-done(((bf16[64,2,1024]{2,1,0:T(2,128)(2,1)}), bf16[1024,2,1024]{2,1,0:T(2,128)(2,1)}) %all-gather.10.cloned.1.call-update) | async-done | bytes 4194320 | tf_op jit(solution)/shard_map/all_gather | solution.py:124
  117.8 11.1 %copy.52 = bf16[1024,2,1024]{0,2,1:T(8,128)(2,1)} copy(bf16[1024,2,1024]{2,1,0:T(2,128)(2,1)} %all-gather.10.cloned.1.call-done) | data formatting | bytes 8388608 | tf_op jit(solution)/shard_map/all_gather | solution.py:124
  128.9 3.8 convolution_convert_fusion
  133.0 2.6 stack.5
  135.6 7.1 all-to-all-start
  142.8 48.4 %reduce-scatter.6.cloned.1.call-done = bf16[128,1024]{1,0:T(8,128)(2,1)} async-done(((bf16[1024,1024]{1,0:T(8,128)(2,1)}), bf16[128,1024]{1,0:T(8,128)(2,1)}) %reduce-scatter.6.cloned.1.call-update) | async-done | bytes 262160 | tf_op jit(solution)/shard_map/reduce_scatter | solution.py:92
  191.2 1.1 convert_reduce_fusion
  193.5 64.6 %all-gather.12.cloned.1.call-done = bf16[1024,1024]{1,0:T(8,128)(2,1)} async-done(((bf16[64,1024]{1,0:T(8,128)(2,1)}), bf16[1024,1024]{1,0:T(8,128)(2,1)}) %all-gather.12.cloned.1.call-update) | async-done | bytes 2097168 | tf_op jit(solution)/shard_map/all_gather | solution.py:123
  258.1 2.3 convolution_convert_fusion.5
  260.4 1.0 copy.56
  261.4 51.6 %all-gather.14.cloned.1.call-done = bf16[1024,1024]{1,0:T(8,128)(2,1)} async-done(((bf16[64,1024]{1,0:T(8,128)(2,1)}), bf16[1024,1024]{1,0:T(8,128)(2,1)}) %all-gather.14.cloned.1.call-update) | async-done | bytes 2097168 | tf_op jit(solution)/shard_map/all_gather | solution.py:125
  313.0 2.3 convolution_convert_fusion.4
  315.3 1.0 copy.58
  316.3 38.9 %all-gather.8.cloned.1.call-done = bf16[1024,1024]{1,0:T(8,128)(2,1)} async-done(((bf16[128,1024]{1,0:T(8,128)(2,1)}), bf16[1024,1024]{1,0:T(8,128)(2,1)}) %all-gather.8.cloned.1.call-update) | async-done | bytes 2097168 | tf_op jit(solution)/shard_map/all_gather | solution.py:101
  355.2 5.8 convolution_convert_fusion.1
  361.3 6.4 copy.54
  367.8 4.0 fusion.96
  371.8 2.5 copy.57
  374.3 2.9 copy.55
  377.2 9.9 %fusion.98 = (f32[16,256]{1,0:T(8,128)S(1)}, f32[16,256,1024]{2,1,0:T(8,128)}) fusion(bf16[256,16,64]{0,2,1:T(8,128)(2,1)S(1)} %bitcast.151, bf16[1024,16,64]{0,2,1:T(8,128)(2,1)} %bitcast.146), kind=kOutput, calls=%fused_computation.110 | convolution fusion | flops 549454848 | bytes 19415040 | tf_op jit(solution)/shard_map/sub | solution.py:30
  387.1 8.1 fusion.99
  395.2 38.2 %fusion.38 = bf16[16,64,1024]{2,1,0:T(8,128)(2,1)} fusion(bf16[256,16,64]{0,2,1:T(8,128)(2,1)S(1)} %bitcast.152, f32[16,256,1024]{2,1,0:T(8,128)} %fusion.99, f32[16,256,1024]{2,1,0:T(8,128)} %get-tuple-element.18, f32[16,256]{1,0:T(8,128)S(1)} %get-tuple-element.17), kind=kOutput, calls=%fused_computation.40 | convolution fusion | flops 567284736 | bytes 36192256 | tf_op jit(solution)/shard_map/hrl,rhd->lhd/dot_general | solution.py:180
  433.3 7.1 fusion.35
  440.5 2.4 pad_maximum_fusion
  442.9 6.5 copy.64
  449.5 1.9 broadcast_select_fusion
  451.4 52.1 %reduce-scatter.10.cloned.1.call-done = bf16[128,2048]{1,0:T(8,128)(2,1)} async-done(((bf16[1024,2048]{1,0:T(8,128)(2,1)}), bf16[128,2048]{1,0:T(8,128)(2,1)}) %reduce-scatter.10.cloned.1.call-update) | async-done | bytes 524304
  503.5 2.1 copy.65
  505.8 8.5 fusion.42
  514.4 2.7 fusion.78
  517.1 10.0 %fusion.95 = (bf16[1024,1,1024]{2,1,0:T(2,128)(2,1)}, bf16[1024,1,1024]{2,1,0:T(2,128)(2,1)}) fusion(bf16[1024,2,1024]{2,1,0:T(2,128)(2,1)} %all-gather.10.cloned.1.call-done), kind=kLoop, calls=%fused_computation.107 | loop fusion | bytes 8388608 | tf_op jit(solution)/shard_map/slice | solution.py:49
  527.1 1.9 collective-permute-start
  529.0 1.5 fusion.45
  530.6 4.5 collective-permute-done
  535.0 111.3 %all-reduce.6.cloned.1.call-done = (bf16[128,1024]{1,0:T(8,128)(2,1)}, bf16[128,2,1024]{0,2,1:T(8,128)(2,1)}) async-done(((bf16[128,1024]{1,0:T(8,128)(2,1)}, bf16[128,2,1024]{0,2,1:T(8,128)(2,1)}), (bf16[128,1024]{1,0:T(8,128)(2,1)}, bf16[128,2,1024]{0,2,1:T(8,128)(2,1)})) %all-reduce.6.cloned.1.call-update) | async-done | bytes 786448 | tf_op jit(solution)/shard_map/psum | solution.py:18
  647.9 3.1 fusion.33
  651.0 3.9 fusion.49
  654.9 272.9 %all-reduce.4.cloned.1.call-done = f32[1024,1024]{1,0:T(8,128)} async-done(((f32[1024,1024]{1,0:T(8,128)}), f32[1024,1024]{1,0:T(8,128)}) %all-reduce.4.cloned.1.call-update) | async-done | bytes 4194320 | tf_op jit(solution)/shard_map/psum | solution.py:171
  928.5 4.8 copy.83
  (62 shorter events, 6.5 us)
Async XLA Ops:
  7.2 348.1 %copy-start = (bf16[1,512,1024]{2,1,0:T(8,128)(2,1)S(1)}, bf16[1,512,1024]{2,1,0:T(8,128)(2,1)}, u32[]{:S(2)}) copy-start(bf16[1,512,1024]{2,1,0:T(8,128)(2,1)} %param.19) | copy-start | bytes 3145732
  7.2 48.2 %all-gather.6.cloned.1.call-start = ((), (), s32[]{:S(2)}) async-start(), calls=%async_computation.4 | async-start | bytes 2359296 | tf_op jit(solution)/shard_map/all_gather | solution.py:89
  11.5 106.4 %all-gather.10.cloned.1.call-start = ((), (), s32[]{:S(2)}) async-start(), calls=%async_computation.8 | async-start | bytes 4456448 | tf_op jit(solution)/shard_map/all_gather | solution.py:124
  12.2 179.0 %reduce-scatter.6.cloned.1.call-start = ((), (), s32[]{:S(2)}) async-start(), calls=%async_computation.5 | async-start | bytes 2359296 | tf_op jit(solution)/shard_map/reduce_scatter | solution.py:92
  62.9 4.3 copy-start.11
  69.3 188.8 %all-gather.12.cloned.1.call-start = ((), (), s32[]{:S(2)}) async-start(), calls=%async_computation.9 | async-start | bytes 2228224 | tf_op jit(solution)/shard_map/all_gather | solution.py:123
  69.9 243.1 %all-gather.14.cloned.1.call-start = ((), (), s32[]{:S(2)}) async-start(), calls=%async_computation.10 | async-start | bytes 2228224 | tf_op jit(solution)/shard_map/all_gather | solution.py:125
  70.5 58.5 %copy-start.12 = (bf16[1,128,1024]{2,1,0:T(8,128)(2,1)S(1)}, bf16[1,128,1024]{2,1,0:T(8,128)(2,1)}, u32[]{:S(2)}) copy-start(bf16[1,128,1024]{2,1,0:T(8,128)(2,1)} %param.20) | copy-start | bytes 786436
  135.6 55.6 %copy-start.2 = (bf16[1,1,128,1024]{3,2,1,0:T(8,128)(2,1)S(1)}, bf16[1,1,128,1024]{3,2,1,0:T(8,128)(2,1)}, u32[]{:S(2)}) copy-start(bf16[1,1,128,1024]{3,2,1,0:T(8,128)(2,1)} %param.13) | copy-start | bytes 786436
  135.6 57.0 %copy-start.14 = (f32[1,1024]{1,0:T(1,128)S(1)}, f32[1,1024]{1,0:T(1,128)}, u32[]{:S(2)}) copy-start(f32[1,1024]{1,0:T(1,128)} %param.17) | copy-start | bytes 12292
  135.6 122.5 %copy-start.8 = (bf16[1,256,1024]{2,1,0:T(8,128)(2,1)S(1)}, bf16[1,256,1024]{2,1,0:T(8,128)(2,1)}, u32[]{:S(2)}) copy-start(bf16[1,256,1024]{2,1,0:T(8,128)(2,1)} %param.21) | copy-start | bytes 1572868
  135.6 225.7 %all-to-all-start = ((bf16[8,128,2048]{1,2,0:T(8,128)(2,1)}), bf16[8,128,2048]{1,2,0:T(8,128)(2,1)}, u32[]{:S(2)}, u32[]{:S(2)}) async-start(bf16[8,128,2048]{1,2,0:T(8,128)(2,1)} %stack.5), calls=%async_computation.2 | async-start | bytes 8388608 | tf_op jit(solution)/shard_map/all_to_all | solution.py:132
  142.7 170.3 %copy-start.6 = (bf16[1,256,1024]{2,1,0:T(8,128)(2,1)S(1)}, bf16[1,256,1024]{2,1,0:T(8,128)(2,1)}, u32[]{:S(2)}) copy-start(bf16[1,256,1024]{2,1,0:T(8,128)(2,1)} %param.25) | copy-start | bytes 1572868
  142.7 212.5 %all-gather.8.cloned.1.call-start = ((), (), s32[]{:S(2)}) async-start(), calls=%async_computation.6 | async-start | bytes 2359296 | tf_op jit(solution)/shard_map/all_gather | solution.py:101
  193.5 256.0 %reduce-scatter.8.cloned.1.call-start = ((), (), s32[]{:S(2)}) async-start(), calls=%async_computation.7 | async-start | bytes 2359296 | tf_op jit(solution)/shard_map/reduce_scatter | solution.py:109
  361.1 142.4 %reduce-scatter.10.cloned.1.call-start = ((), (), s32[]{:S(2)}) async-start(), calls=%async_computation.12 | async-start | bytes 4718592
  371.8 5.4 copy-start.10
  377.2 9.9 %copy-start.4 = (bf16[256,1024]{0,1:T(8,128)(2,1)S(1)}, bf16[256,1024]{0,1:T(8,128)(2,1)}, u32[]{:S(2)}) copy-start(bf16[256,1024]{0,1:T(8,128)(2,1)} %copy.58) | copy-start | bytes 1572868
  433.3 7.1 copy-start.5
  449.4 196.9 %all-reduce.6.cloned.1.call-start = ((), (), s32[]{:S(2)}) async-start(), calls=%async_computation.13 | async-start | bytes 1572864 | tf_op jit(solution)/shard_map/psum | solution.py:18
  505.6 8.8 copy-start.7
  505.6 422.2 %all-reduce.4.cloned.1.call-start = ((), (), s32[]{:S(2)}) async-start(), calls=%async_computation.11 | async-start | bytes 8388608 | tf_op jit(solution)/shard_map/psum | solution.py:171
  517.1 10.0 %copy-start.13 = (bf16[128,1024]{1,0:T(8,128)(2,1)S(1)}, bf16[128,1024]{1,0:T(8,128)(2,1)}, u32[]{:S(2)}) copy-start(bf16[128,1024]{1,0:T(8,128)(2,1)} %get-tuple-element.8) | copy-start | bytes 786436
  517.1 11.9 %copy-start.3 = (bf16[1024,1024]{1,0:T(8,128)(2,1)S(1)}, bf16[1024,1024]{1,0:T(8,128)(2,1)}, u32[]{:S(2)}) copy-start(bf16[1024,1024]{1,0:T(8,128)(2,1)} %all-gather.14.cloned.1.call-done) | copy-start | bytes 6291460
  517.1 11.9 %copy-start.9 = (bf16[1,256,1024]{2,1,0:T(8,128)(2,1)S(1)}, bf16[1,256,1024]{2,1,0:T(8,128)(2,1)}, u32[]{:S(2)}) copy-start(bf16[1,256,1024]{2,1,0:T(8,128)(2,1)} %param.21) | copy-start | bytes 1572868
  527.1 8.0 collective-permute-start
  927.8 5.5 copy-start.1
Sparse Core Ops, SparseCore 0:
  11.6 43.7 all-gather.5
  58.2 59.6 all-gather.9
  120.4 70.7 reduce-scatter.5
  193.8 64.2 all-gather.11
  260.7 52.2 all-gather.13
  315.2 39.9 all-gather.7
  361.2 41.4 reduce-scatter.7
  449.5 53.8 reduce-scatter.9
  506.8 139.5 all-reduce.5
  651.7 276.0 all-reduce.3
